TPU v7x, 256 devices: a whole 4x4x8 slice. The times are simulated.
256 devices in a mesh: facet: 16 (over y, x_lo, core), team: 8 (over z), sub: 2 (over x_hi).
Axes of the slice: x: 4 (x_hi: 2, x_lo: 2; x = x_hi * 2 + x_lo), y: 4, z: 8, core: 2. Of those that a mesh axis runs over, the one named last changes fastest.
Arguments:
- facet_rows: bfloat16 [16, 2, 64, 4096], P('facet', None, 'team'), may hold values from -6 to 6
- sub_offsets: int32 [32, 2], replicated, may hold values from 0 to 4095
- facet_offsets: int32 [16, 2], replicated, may hold values from 0 to 4095
- aterm: bfloat16 [16, 2, 256, 256], P('facet'), may hold values from 0.29882812 to 3
- cells: int32 [16, 2, 8, 2, 256], P('facet', None, 'team'), may hold values from 0 to 1023
- observed: bfloat16 [16, 2, 8, 2, 256], P('facet', None, 'team'), may hold values from -6 to 6
- weights: bfloat16 [16, 2, 8, 256], P('facet', None, 'team'), may hold values from 0.29882812 to 3
- counts: int32 [16, 2, 8], replicated, may hold values from 1 to 256, as said below
Outputs:
- facet_update: float32 [16, 2, 64, 4096], P('facet', None, 'team', 'sub')
Inputs may be any that keep to these rules, and one draw needn't show every extreme that they name: Slots 0 to counts[a, b, t] - 1 are live. For every a and t one of the two subgrids with indices [a, 0] and [a, 1] has at most 64 live slots, and which of the two it is does not change with t.
All inputs are finite; a program needn't handle non-finite values.
Results may differ from a plain program's by a relative error of at most 0.019.
Values may be sent and summed in bfloat16 or wider, within the bound.
No kernel may reach another device: no remote copies, remote signals or barrier semaphores. Data moves between devices by JAX's collectives and lax.ppermute only.
A program may use at most 64 MiB of HBM per device.

v0:
```python
import math
import jax
import jax.numpy as jnp
from jax import lax
from jax.sharding import PartitionSpec as P

L = 4096
M = 128
SG = 256
VB = 256
TWO_PI = 2.0 * math.pi
HIGHEST = lax.Precision.HIGHEST


def cut_along(shard, dim, peers):
    before, after = (shard.shape[:dim], shard.shape[dim + 1 :])
    return jnp.moveaxis(shard.reshape(*before, peers, -1, *after), dim, 0)


def sum_at_owner(shard, axis, dim):
    peers = lax.axis_size(axis)
    parts = lax.all_to_all(cut_along(shard, dim, peers), axis, 0, 0, tiled=True)
    return jnp.sum(parts, axis=0)


def in_order(parts, dim):
    parts = jnp.moveaxis(parts, 0, dim)
    lengths = parts.shape
    return parts.reshape(*lengths[:dim], lengths[dim] * lengths[dim + 1], *lengths[dim + 2 :])


def from_everyone(shard, axis):
    copies = jnp.broadcast_to(shard, (lax.axis_size(axis), *shard.shape))
    return lax.all_to_all(copies, axis, split_axis=0, concat_axis=0, tiled=True)


def collect(shard, axis, dim):
    return in_order(from_everyone(shard, axis), dim)


def over_copies(shard, axis):
    return from_everyone(shard, axis).astype(jnp.float32).sum(axis=0)


def partner(value, axis, stride):
    mask = 2**stride
    pairs = [(source, source ^ mask) for source in range(lax.axis_size(axis))]
    return lax.ppermute(value, axis, pairs)


def angles(left_ints, right_ints, period):
    return (left_ints * right_ints % period).astype(jnp.float32) * (TWO_PI / period)


def transform_tables():
    columns = jnp.arange(L, dtype=jnp.int32)
    frequency = jnp.arange(M, dtype=jnp.int32)
    angle_grid = angles(columns[:, None], frequency[None, :], L)
    cos_part = jnp.cos(angle_grid)
    sin_part = jnp.sin(angle_grid)
    spec_re = (cos_part / math.sqrt(L)).astype(jnp.bfloat16)
    spec_im = (-sin_part / math.sqrt(L)).astype(jnp.bfloat16)
    forward = jnp.concatenate(
        [jnp.concatenate([spec_re, spec_im], 1), jnp.concatenate([-spec_im, spec_re], 1)], 0
    )
    back_re = (cos_part.T / math.sqrt(M)).astype(jnp.bfloat16)
    back_im = (sin_part.T / math.sqrt(M)).astype(jnp.bfloat16)
    backward = jnp.concatenate(
        [jnp.concatenate([back_re, back_im], 1), jnp.concatenate([-back_im, back_re], 1)], 0
    )
    return (forward, backward)


def subgrid_table(size_sub):
    freq_ids = jnp.arange(M, dtype=jnp.int32)
    cell_ids = jnp.arange(size_sub, dtype=jnp.int32)
    angle_grid = angles(freq_ids[:, None], cell_ids[None, :], size_sub)
    factor = 1.0 / math.sqrt(M)
    return (jnp.cos(angle_grid) * factor, jnp.sin(angle_grid) * factor)


def facet_phase(row_ids, facet_offsets):
    col_ids = jnp.arange(M, dtype=jnp.int32)
    along_rows = row_ids[:, None] * facet_offsets[None, :, 0] % L
    along_cols = col_ids[None, :] * facet_offsets[:, 1:2] % L
    angle_grid = ((along_rows[:, :, None] + along_cols[None, :, :]) % L).astype(jnp.float32) * (
        TWO_PI / L
    )
    return (jnp.cos(angle_grid), jnp.sin(angle_grid))


def hdot(left, right):
    return jnp.dot(left, right, precision=HIGHEST, preferred_element_type=jnp.float32)


def hsum(form, left, right):
    return jnp.einsum(form, left, right, precision=HIGHEST, preferred_element_type=jnp.float32)


def to_image(assembled, k_re, k_im):
    grid_re = assembled[:, 0]
    grid_im = assembled[:, 1]
    temp_re = hdot(k_re.T, grid_re) - hdot(k_im.T, grid_im)
    temp_im = hdot(k_re.T, grid_im) + hdot(k_im.T, grid_re)
    image_re = hdot(temp_re, k_re) - hdot(temp_im, k_im)
    image_im = hdot(temp_re, k_im) + hdot(temp_im, k_re)
    return (image_re, image_im)


def to_return(grid, weight_map, k_re, k_im):
    size_sub = weight_map.shape[0]
    grid_re = grid[:, :size_sub] * weight_map / size_sub
    grid_im = grid[:, size_sub:] * weight_map / size_sub
    temp_re = hdot(k_re, grid_re) + hdot(k_im, grid_im)
    temp_im = hdot(k_re, grid_im) - hdot(k_im, grid_re)
    out_re = hdot(temp_re, k_re.T) + hdot(temp_im, k_im.T)
    out_im = hdot(temp_im, k_re.T) - hdot(temp_re, k_im.T)
    return jnp.stack([out_re, out_im], 1)


def degrid_block(weighted, cell_pair, observed_pair, weight, live):
    size_sub = weighted.shape[1]
    block_len = cell_pair.shape[1]
    index = jnp.arange(size_sub, dtype=jnp.int32)
    row_angle = angles(cell_pair[0][:, None], index[None, :], 4 * size_sub)
    col_angle = angles(cell_pair[1][:, None], index[None, :], 4 * size_sub)
    row_cos = jnp.cos(row_angle).astype(jnp.bfloat16)
    row_sin = jnp.sin(row_angle).astype(jnp.bfloat16)
    col_cos = jnp.cos(col_angle).astype(jnp.bfloat16)
    col_sin = jnp.sin(col_angle).astype(jnp.bfloat16)
    col_stack = jnp.concatenate([col_cos, col_sin], 0)
    products = jnp.einsum("jk,ik->ji", col_stack, weighted, preferred_element_type=jnp.float32)
    part_re = products[:block_len, :size_sub] + products[block_len:, size_sub:]
    part_im = products[:block_len, size_sub:] - products[block_len:, :size_sub]
    cos_rows = row_cos.astype(jnp.float32)
    sin_rows = row_sin.astype(jnp.float32)
    cos_cols = col_cos.astype(jnp.float32)
    sin_cols = col_sin.astype(jnp.float32)
    pred_re = jnp.sum(cos_rows * part_re + sin_rows * part_im, 1) / size_sub
    pred_im = jnp.sum(cos_rows * part_im - sin_rows * part_re, 1) / size_sub
    res_re = live * weight * (observed_pair[0] - pred_re)
    res_im = live * weight * (observed_pair[1] - pred_im)
    spread_re = (res_re[:, None] * cos_cols - res_im[:, None] * sin_cols).astype(jnp.bfloat16)
    spread_im = (res_re[:, None] * sin_cols + res_im[:, None] * cos_cols).astype(jnp.bfloat16)
    right = jnp.concatenate(
        [jnp.concatenate([spread_re, spread_im], 1), jnp.concatenate([-spread_im, spread_re], 1)], 0
    )
    left = jnp.concatenate([row_cos, row_sin], 0)
    return jnp.einsum("ji,jk->ik", left, right, preferred_element_type=jnp.float32)


def weigh_image(assembled, weight_map, k_re, k_im):
    image_re, image_im = to_image(assembled, k_re, k_im)
    return jnp.concatenate(
        [
            (weight_map * image_re).astype(jnp.bfloat16),
            (weight_map * image_im).astype(jnp.bfloat16),
        ],
        0,
    )


def local(facet_rows, sub_offsets, facet_offsets, aterm, cells, observed, weights, counts):
    n_facet = lax.axis_size("facet")
    n_team = lax.axis_size("team")
    n_sub = lax.axis_size("sub")
    my_facet = lax.axis_index("facet")
    my_team = lax.axis_index("team")
    my_side = lax.axis_index("sub")
    rows_dev = facet_rows.shape[2]
    rows_all = rows_dev * n_team
    norm = 1.0 / math.sqrt(n_facet)
    share = M // n_team
    forward, backward = transform_tables()
    k_re, k_im = subgrid_table(SG)
    sub_ids = jnp.arange(n_facet, dtype=jnp.int32) * n_sub + my_side
    shifts = sub_offsets[sub_ids, 0]
    tunings = sub_offsets[sub_ids, 1]
    columns = jnp.arange(L, dtype=jnp.int32)
    mod_angle = angles(tunings[:, None], columns[None, :], L)
    mod_cos = jnp.cos(mod_angle)[:, None, :]
    mod_sin = jnp.sin(mod_angle)[:, None, :]
    rows_re = facet_rows[0, 0].astype(jnp.float32)[None]
    rows_im = facet_rows[0, 1].astype(jnp.float32)[None]
    mod_re = (rows_re * mod_cos + rows_im * mod_sin).astype(jnp.bfloat16)
    mod_im = (rows_im * mod_cos - rows_re * mod_sin).astype(jnp.bfloat16)
    stacked = jnp.concatenate([mod_re, mod_im], 2).reshape(n_facet * rows_dev, 2 * L)
    spectrum = jnp.dot(stacked, forward, preferred_element_type=jnp.float32).reshape(
        n_facet, rows_dev, 2, M
    )
    row_ids = my_team * rows_dev + jnp.arange(rows_dev, dtype=jnp.int32)
    out_ids = jnp.arange(M, dtype=jnp.int32)
    w_angle = angles(
        out_ids[None, :, None] + shifts[:, None, None], row_ids[None, None, :], rows_all
    )
    w_re = jnp.cos(w_angle) / math.sqrt(rows_all)
    w_im = -jnp.sin(w_angle) / math.sqrt(rows_all)
    part_re = w_re
    part_im = w_im
    real_out = hsum("fpr,frm->pfm", part_re, spectrum[:, :, 0]) - hsum(
        "fpr,frm->pfm", part_im, spectrum[:, :, 1]
    )
    imag_out = hsum("fpr,frm->pfm", part_re, spectrum[:, :, 1]) + hsum(
        "fpr,frm->pfm", part_im, spectrum[:, :, 0]
    )
    mine = sum_at_owner(jnp.stack([real_out, imag_out], 2), "team", 0)
    received = lax.all_to_all(mine, "facet", split_axis=1, concat_axis=1, tiled=True)
    block_rows = received.shape[0]
    phase_cos, phase_sin = facet_phase(
        my_team * share + jnp.arange(block_rows, dtype=jnp.int32), facet_offsets
    )
    grid_re = jnp.sum(phase_cos * received[:, :, 0] - phase_sin * received[:, :, 1], 1) * norm
    grid_im = jnp.sum(phase_cos * received[:, :, 1] + phase_sin * received[:, :, 0], 1) * norm
    assembled = collect(jnp.stack([grid_re, grid_im], 1), "team", 0)
    maps = aterm[0].astype(jnp.float32)
    own_map = lax.dynamic_index_in_dim(maps, my_side, 0, keepdims=False)
    weighted = weigh_image(assembled, own_map, k_re, k_im)
    own_cells = cells[0, :, 0]
    own_obs = observed[0, :, 0]
    own_weights = weights[0, :, 0]
    zero_int = jnp.zeros((), jnp.int32)
    lane_ids = jnp.arange(VB, dtype=jnp.int32)
    empty_grid = jnp.zeros((SG, 2 * SG), jnp.float32)

    def block_term(side, block, image_stack):
        start = block * VB
        cell_pair = lax.dynamic_slice(own_cells, (side, zero_int, start), (1, 2, VB))[0]
        obs_pair = lax.dynamic_slice(own_obs, (side, zero_int, start), (1, 2, VB))[0].astype(
            jnp.float32
        )
        weight = lax.dynamic_slice(own_weights, (side, start), (1, VB))[0].astype(jnp.float32)
        live = (start + lane_ids < counts[my_facet, side, my_team]).astype(jnp.float32)
        return degrid_block(image_stack, cell_pair, obs_pair, weight, live)

    own_blocks = (counts[my_facet, my_side, my_team] + VB - 1) // VB

    def own_step(block, total):
        return total + block_term(my_side, block, weighted)

    grid = lax.fori_loop(0, own_blocks, own_step, empty_grid)
    returned = to_return(grid, own_map, k_re, k_im)
    total_back = over_copies(returned.astype(jnp.bfloat16), "team").astype(jnp.float32)
    block_rows = total_back.shape[0]
    phase_cos, phase_sin = facet_phase(jnp.arange(block_rows, dtype=jnp.int32), facet_offsets)
    back_re = (phase_cos * total_back[:, None, 0] + phase_sin * total_back[:, None, 1]) * norm
    back_im = (phase_cos * total_back[:, None, 1] - phase_sin * total_back[:, None, 0]) * norm
    arrived = lax.all_to_all(
        jnp.stack([back_re, back_im], 2).astype(jnp.bfloat16),
        "facet",
        split_axis=1,
        concat_axis=1,
        tiled=True,
    ).astype(jnp.float32)
    part_re = w_re
    part_im = w_im
    fold_re = hsum("fpr,pfm->frm", part_re, arrived[:, :, 0]) + hsum(
        "fpr,pfm->frm", part_im, arrived[:, :, 1]
    )
    fold_im = hsum("fpr,pfm->frm", part_re, arrived[:, :, 1]) - hsum(
        "fpr,pfm->frm", part_im, arrived[:, :, 0]
    )
    folded = jnp.stack([fold_re, fold_im], 2)
    folded_stack = folded.astype(jnp.bfloat16).reshape(n_facet * rows_dev, 2 * M)
    half = L // n_sub
    col_start = my_side * half
    other_stack = partner(folded_stack, "sub", 0)
    both_stacks = jnp.concatenate([folded_stack, other_stack], 0)
    back_half = jnp.concatenate(
        [
            lax.dynamic_slice_in_dim(backward, col_start, half, 1),
            lax.dynamic_slice_in_dim(backward, L + col_start, half, 1),
        ],
        1,
    )
    spectra_half = jnp.dot(both_stacks, back_half, preferred_element_type=jnp.float32).reshape(
        2 * n_facet, rows_dev, 2, half
    )
    other_ids = jnp.arange(n_facet, dtype=jnp.int32) * n_sub + (1 - my_side)
    all_tunings = jnp.concatenate([tunings, sub_offsets[other_ids, 1]], 0)
    half_cols = col_start + jnp.arange(half, dtype=jnp.int32)
    half_angle = angles(all_tunings[:, None], half_cols[None, :], L)
    half_cos = jnp.cos(half_angle)[:, None, :]
    half_sin = jnp.sin(half_angle)[:, None, :]
    update_re = jnp.sum(spectra_half[:, :, 0] * half_cos - spectra_half[:, :, 1] * half_sin, 0)
    update_im = jnp.sum(spectra_half[:, :, 1] * half_cos + spectra_half[:, :, 0] * half_sin, 0)
    return jnp.stack([update_re, update_im], 0)[None]


def solution(mesh):
    placed = (
        P("facet", None, "team", None),
        P(),
        P(),
        P("facet", None, None, None),
        P("facet", None, "team", None, None),
        P("facet", None, "team", None, None),
        P("facet", None, "team", None),
        P(),
    )
    return jax.shard_map(
        local,
        mesh=mesh,
        in_specs=placed,
        out_specs=P("facet", None, "team", "sub"),
        check_vma=False,
    )
```

profile of v0, /device:TPU:1, one launch (start us, length us, event | category | flops | bytes accessed | tf_op | source)
XLA Modules:
  0.0 229.4 jit_solution(1294391637697271506)
XLA Ops:
  0.0 8.5 %multiply_convert_fusion.2 = (bf16[4096,128]{0,1:T(8,128)(2,1)S(1)}, bf16[4096,128]{0,1:T(8,128)(2,1)S(1)}) fusion(), kind=kLoop, calls=%fused_computation.82 | loop fusion | flops 9961472 | bytes 2097152 | tf_op jit(solution)/shard_map/convert_element_type | solution.py:62
  8.5 7.9 %fusion.68 = bf16[4096,128]{0,1:T(8,128)(2,1)S(1)} fusion(), kind=kLoop, calls=%fused_computation.135 | loop fusion | flops 10485760 | bytes 1048576 | tf_op jit(solution)/shard_map/neg | solution.py:64
  16.4 0.7 gather_fusion.1
  17.7 1.9 fusion.126
  19.5 1.5 bitcast_convert_fusion.1
  21.1 1.2 gather_fusion
  23.0 18.1 %maximum_maximum_fusion = bf16[8192,256]{0,1:T(8,128)(2,1)S(1)} fusion(bf16[4096,128]{0,1:T(8,128)(2,1)S(1)} %get-tuple-element.313, bf16[4096,128]{0,1:T(8,128)(2,1)S(1)} %fusion.68, bf16[4096,128]{0,1:T(8,128)(2,1)S(1)} %get-tuple-element.312), kind=kLoop, calls=%fused_computation.51 | loop fusion | flops 16777216 | bytes 7340032 | tf_op jit(solution)/shard_map/concatenate | solution.py:63
  41.6 1.5 fusion.36
  43.1 1.9 fusion.141
  45.0 1.9 fusion.142
  47.0 1.9 convolution_subtract_fusion
  48.9 1.9 convolution_add_fusion.1
  51.1 1.5 copy.42
  52.6 9.1 %all-to-all-start = ((f32[8,16,16,2,128]{4,1,2,3,0:T(8,128)}), f32[8,16,16,2,128]{4,1,2,3,0:T(8,128)S(1)}, u32[]{:S(2)}, u32[]{:S(2)}) async-start(f32[8,16,16,2,128]{4,1,2,3,0:T(8,128)} %copy.42), calls=%async_computation | async-start | bytes 4194304 | tf_op jit(solution)/shard_map/all_to_all | solution.py:22
  61.8 0.7 gather_fusion.2
  62.8 7.9 %fusion.69 = bf16[128,4096]{1,0:T(8,128)(2,1)S(1)} fusion(), kind=kLoop, calls=%fused_computation.136 | loop fusion | flops 9961472 | bytes 1048576 | tf_op jit(solution)/shard_map/neg | solution.py:69
  70.7 39.6 %all-to-all-done = f32[8,16,16,2,128]{4,1,2,3,0:T(8,128)S(1)} async-done(((f32[8,16,16,2,128]{4,1,2,3,0:T(8,128)}), f32[8,16,16,2,128]{4,1,2,3,0:T(8,128)S(1)}, u32[]{:S(2)}, u32[]{:S(2)}) %all-to-all-start) | async-done | bytes 2097184 | tf_op jit(solution)/shard_map/all_to_all | solution.py:22
  110.4 0.7 copy.34
  111.1 9.4 %all-to-all-start.1 = ((f32[16,16,2,128]{3,0,2,1:T(8,128)}), f32[16,16,2,128]{3,0,2,1:T(8,128)S(1)}, u32[]{:S(2)}, u32[]{:S(2)}) async-start(f32[16,16,2,128]{3,0,2,1:T(8,128)} %copy.34), calls=%async_computation.1 | async-start | bytes 524288 | tf_op jit(solution)/shard_map/all_to_all | solution.py:207
  120.6 1.3 dynamic_slice.40
  122.6 5.0 %all-to-all-done.1 = f32[16,16,2,128]{3,0,2,1:T(8,128)S(1)} async-done(((f32[16,16,2,128]{3,0,2,1:T(8,128)}), f32[16,16,2,128]{3,0,2,1:T(8,128)S(1)}, u32[]{:S(2)}, u32[]{:S(2)}) %all-to-all-start.1) | async-done | bytes 262176 | tf_op jit(solution)/shard_map/all_to_all | solution.py:207
  128.3 0.7 broadcast_in_dim.9
  129.0 3.5 %all-to-all-start.2 = ((f32[8,16,2,128]{3,2,1,0:T(2,128)}), f32[8,16,2,128]{3,2,1,0:T(2,128)S(1)}, u32[]{:S(2)}, u32[]{:S(2)}) async-start(f32[8,16,2,128]{3,2,1,0:T(2,128)} %broadcast_in_dim.9), calls=%async_computation.2 | async-start | bytes 262144 | tf_op jit(solution)/shard_map/all_to_all | solution.py:34
  132.5 1.1 cosine_convert_fusion.2
  133.6 6.5 %all-to-all-done.2 = f32[8,16,2,128]{3,2,1,0:T(2,128)S(1)} async-done(((f32[8,16,2,128]{3,2,1,0:T(2,128)}), f32[8,16,2,128]{3,2,1,0:T(2,128)S(1)}, u32[]{:S(2)}, u32[]{:S(2)}) %all-to-all-start.2) | async-done | bytes 131104 | tf_op jit(solution)/shard_map/all_to_all | solution.py:34
  140.3 0.8 fusion.137
  141.1 0.8 fusion.139
  142.0 0.8 convolution_subtract_fusion.3
  142.8 0.9 fusion.138
  143.7 0.9 fusion.140
  144.6 0.8 convolution_add_fusion.4
  145.4 0.9 fusion.51
  146.3 0.9 fusion.52
  147.5 1.2 fusion.73
  148.7 5.3 %while.15 = (s32[]{:T(128)}, f32[256,512]{1,0:T(8,128)S(1)}, s32[]{:T(128)}, s32[1,2,256]{2,1,0:T(2,128)S(1)}, s32[1,1,1]{2,1,0:T(1,128)}, /*index=5*/bf16[1,256...) while((s32[]{:T(128)}, f32[256,512]{1,0:T(8,128)S(1)}, ...), condition=%wide.region_6.7_spmd.clone, body=%wide.region_5.6_spmd.clone.sunk | while | flops 141363712 | bytes 2383489 | solution.py:240
  149.4 1.3 fusion.327
  150.7 1.3 fusion.328
  152.0 1.3 cosine_convert_fusion.5
  154.1 0.8 fusion.108
  154.9 0.8 fusion.104
  155.7 0.8 convolution_add_fusion.3
  156.6 0.8 fusion.136
  157.3 0.8 convolution_subtract_fusion.2
  158.2 0.8 fusion.135
  158.9 0.8 fusion.58
  159.7 0.8 fusion.57
  160.5 0.9 broadcast_in_dim.10
  161.4 4.1 %all-to-all-start.3 = ((bf16[8,128,2,128]{3,1,2,0:T(8,128)(2,1)}), bf16[8,128,2,128]{3,1,2,0:T(8,128)(2,1)}, u32[]{:S(2)}, u32[]{:S(2)}) async-start(bf16[8,128,2,128]{3,1,2,0:T(8,128)(2,1)} %broadcast_in_dim.10), calls=%async_computation.3 | async-start | bytes 1048576 | tf_op jit(solution)/shard_map/all_to_all | solution.py:34
  165.5 1.9 fusion.120
  167.4 8.5 %multiply_convert_fusion = (bf16[128,4096]{1,0:T(8,128)(2,1)S(1)}, bf16[128,4096]{1,0:T(8,128)(2,1)S(1)}) fusion(), kind=kLoop, calls=%fused_computation.78 | loop fusion | flops 9437184 | bytes 2097152 | tf_op jit(solution)/shard_map/convert_element_type | solution.py:67
  175.9 4.8 %all-to-all-done.3 = bf16[8,128,2,128]{3,1,2,0:T(8,128)(2,1)} async-done(((bf16[8,128,2,128]{3,1,2,0:T(8,128)(2,1)}), bf16[8,128,2,128]{3,1,2,0:T(8,128)(2,1)}, u32[]{:S(2)}, u32[]{:S(2)}) %all-to-all-start.3) | async-done | bytes 524320 | tf_op jit(solution)/shard_map/all_to_all | solution.py:34
  180.7 1.1 convert_reduce_fusion
  181.8 4.8 %multiply_convert_fusion.5 = (bf16[128,16,1,128]{3,0,2,1:T(8,128)(2,1)S(1)}, bf16[128,16,1,128]{3,0,2,1:T(8,128)(2,1)S(1)}) fusion(f32[128,128]{1,0:T(8,128)S(1)} %get-tuple-element.295, f32[128,128]{1,0:T(8,128)S(1)} %get-tuple-element.294, s32[16,128]{1,0:T(8,128)S(1)} %add_select_fusion.15, s32[128,16]{0,1:T(8,128)S(1)} %add_select_fusion.16), kind=kLoop, calls=%fused_computation.124 | loop fusion | flops 6291456 | bytes 1196032 | tf_op jit(solution)/shard_map/convert.7
  186.7 1.1 pad_maximum_fusion.1
  187.7 8.2 %all-to-all-start.4 = ((bf16[128,16,2,128]{3,0,2,1:T(8,128)(2,1)}), bf16[128,16,2,128]{3,0,2,1:T(8,128)(2,1)}, u32[]{:S(2)}, u32[]{:S(2)}) async-start(bf16[128,16,2,128]{3,0,2,1:T(8,128)(2,1)} %pad_maximum_fusion.1), calls=%async_computation.4 | async-start | bytes 2097152 | tf_op jit(solution)/shard_map/all_to_all | solution.py:247
  196.0 18.6 %maximum_maximum_fusion.1 = bf16[256,8192]{1,0:T(8,128)(2,1)} fusion(bf16[128,4096]{1,0:T(8,128)(2,1)S(1)} %get-tuple-element.315, bf16[128,4096]{1,0:T(8,128)(2,1)S(1)} %fusion.69, bf16[128,4096]{1,0:T(8,128)(2,1)S(1)} %get-tuple-element.314), kind=kLoop, calls=%fused_computation.52 | loop fusion | flops 16777216 | bytes 7340032 | tf_op jit(solution)/shard_map/concatenate | solution.py:68
  214.5 1.8 fusion.66
  216.3 1.8 fusion.67
  218.1 1.8 fusion.60
  219.9 1.8 fusion.59
  221.6 2.5 %collective-permute-start = (bf16[128,256]{1,0:T(8,128)(2,1)S(1)}, bf16[128,256]{1,0:T(8,128)(2,1)S(1)}, u32[]{:S(2)}, u32[]{:S(2)}) collective-permute-start(bf16[128,256]{1,0:T(8,128)(2,1)S(1)} %copy_bitcast_fusion), channel_id=1, source_target_pairs={{0,1},{1,0},{2,3},{3,2},{4,5},{5,4},{6,7},{7,6},{8,9},{9,8},{10,11... | collective-permute-start | bytes 196616 | tf_op jit(solution)/shard_map/ppermute | solution.py:48
  224.2 1.7 constant_dynamic-slice_fusion.1
  225.9 1.1 collective-permute-done
  227.0 0.7 fusion.39
  (63 shorter events, 6.2 us)
Async XLA Ops:
  0.0 62.5 %copy-start = (s32[1,2,1,2,256]{4,3,2,1,0:T(2,128)S(1)}, s32[1,2,1,2,256]{4,3,2,1,0:T(2,128)}, u32[]{:S(2)}) copy-start(s32[1,2,1,2,256]{4,3,2,1,0:T(2,128)} %param.14) | copy-start | bytes 12292
  0.0 16.4 %copy-start.1 = (s32[32,2]{0,1:T(2,128)S(1)}, s32[32,2]{0,1:T(2,128)}, u32[]{:S(2)}) copy-start(s32[32,2]{0,1:T(2,128)} %param.11) | copy-start | bytes 772
  17.1 0.6 copy-start.7
  23.0 25.9 %copy-start.5 = (s32[8]{0:T(128)}, s32[8]{0:T(128)S(1)}, u32[]{:S(2)}) copy-start(s32[8]{0:T(128)S(1)} %iota_add_fusion.4) | copy-start | bytes 100
  23.0 18.1 %copy-start.3 = (f32[16,4096]{1,0:T(8,128)S(1)}, f32[16,4096]{1,0:T(8,128)}, u32[]{:S(2)}) copy-start(f32[16,4096]{1,0:T(8,128)} %get-tuple-element.309) | copy-start | bytes 786436
  23.0 18.1 %copy-start.4 = (f32[8,4096]{1,0:T(8,128)S(1)}, f32[8,4096]{1,0:T(8,128)}, u32[]{:S(2)}) copy-start(f32[8,4096]{1,0:T(8,128)} %get-tuple-element.299) | copy-start | bytes 393220
  52.6 9.9 %copy-start.9 = (bf16[1,2,1,256]{3,1,2,0:T(2,128)(2,1)S(1)}, bf16[1,2,1,256]{3,1,2,0:T(2,128)(2,1)}, u32[]{:S(2)}) copy-start(bf16[1,2,1,256]{3,1,2,0:T(2,128)(2,1)} %param.16) | copy-start | bytes 3076
  52.6 9.9 %copy-start.11 = (bf16[1,2,1,2,256]{4,3,2,1,0:T(2,128)(2,1)S(1)}, bf16[1,2,1,2,256]{4,3,2,1,0:T(2,128)(2,1)}, u32[]{:S(2)}) copy-start(bf16[1,2,1,2,256]{4,3,2,1,0:T(2,128)(2,1)} %param.15) | copy-start | bytes 6148
  52.6 9.9 %copy-start.10 = (s32[16,2]{0,1:T(2,128)S(1)}, s32[16,2]{0,1:T(2,128)}, u32[]{:S(2)}) copy-start(s32[16,2]{0,1:T(2,128)} %param.12) | copy-start | bytes 388
  52.6 57.6 %all-to-all-start = ((f32[8,16,16,2,128]{4,1,2,3,0:T(8,128)}), f32[8,16,16,2,128]{4,1,2,3,0:T(8,128)S(1)}, u32[]{:S(2)}, u32[]{:S(2)}) async-start(f32[8,16,16,2,128]{4,1,2,3,0:T(8,128)} %copy.42), calls=%async_computation | async-start | bytes 4194304 | tf_op jit(solution)/shard_map/all_to_all | solution.py:22
  62.8 57.8 %copy-start.8 = (s32[16]{0:T(128)S(1)}, s32[16]{0:T(128)}, u32[]{:S(2)}) copy-start(s32[16]{0:T(128)} %copy-done.7) | copy-start | bytes 196
  111.1 16.5 %all-to-all-start.1 = ((f32[16,16,2,128]{3,0,2,1:T(8,128)}), f32[16,16,2,128]{3,0,2,1:T(8,128)S(1)}, u32[]{:S(2)}, u32[]{:S(2)}) async-start(f32[16,16,2,128]{3,0,2,1:T(8,128)} %copy.34), calls=%async_computation.1 | async-start | bytes 524288 | tf_op jit(solution)/shard_map/all_to_all | solution.py:207
  129.0 16.5 %copy-start.12 = (bf16[1,2,256,256]{3,2,1,0:T(8,128)(2,1)S(1)}, bf16[1,2,256,256]{3,2,1,0:T(8,128)(2,1)}, u32[]{:S(2)}) copy-start(bf16[1,2,256,256]{3,2,1,0:T(8,128)(2,1)} %param.13) | copy-start | bytes 786436
  129.0 11.2 %all-to-all-start.2 = ((f32[8,16,2,128]{3,2,1,0:T(2,128)}), f32[8,16,2,128]{3,2,1,0:T(2,128)S(1)}, u32[]{:S(2)}, u32[]{:S(2)}) async-start(f32[8,16,2,128]{3,2,1,0:T(2,128)} %broadcast_in_dim.9), calls=%async_computation.2 | async-start | bytes 262144 | tf_op jit(solution)/shard_map/all_to_all | solution.py:34
  161.4 19.3 %all-to-all-start.3 = ((bf16[8,128,2,128]{3,1,2,0:T(8,128)(2,1)}), bf16[8,128,2,128]{3,1,2,0:T(8,128)(2,1)}, u32[]{:S(2)}, u32[]{:S(2)}) async-start(bf16[8,128,2,128]{3,1,2,0:T(8,128)(2,1)} %broadcast_in_dim.10), calls=%async_computation.3 | async-start | bytes 1048576 | tf_op jit(solution)/shard_map/all_to_all | solution.py:34
  187.7 26.8 %all-to-all-start.4 = ((bf16[128,16,2,128]{3,0,2,1:T(8,128)(2,1)}), bf16[128,16,2,128]{3,0,2,1:T(8,128)(2,1)}, u32[]{:S(2)}, u32[]{:S(2)}) async-start(bf16[128,16,2,128]{3,0,2,1:T(8,128)(2,1)} %pad_maximum_fusion.1), calls=%async_computation.4 | async-start | bytes 2097152 | tf_op jit(solution)/shard_map/all_to_all | solution.py:247
  195.9 18.6 %copy-start.6 = (s32[8]{0:T(128)S(1)}, s32[8]{0:T(128)}, u32[]{:S(2)}) copy-start(s32[8]{0:T(128)} %copy-done.5) | copy-start | bytes 100
  221.6 5.3 %collective-permute-start = (bf16[128,256]{1,0:T(8,128)(2,1)S(1)}, bf16[128,256]{1,0:T(8,128)(2,1)S(1)}, u32[]{:S(2)}, u32[]{:S(2)}) collective-permute-start(bf16[128,256]{1,0:T(8,128)(2,1)S(1)} %copy_bitcast_fusion), channel_id=1, source_target_pairs={{0,1},{1,0},{2,3},{3,2},{4,5},{5,4},{6,7},{7,6},{8,9},{9,8},{10,11... | collective-permute-start | bytes 196616 | tf_op jit(solution)/shard_map/ppermute | solution.py:48
  227.0 1.0 copy-start.2
where the time goes:
time: 233 us; the launch traced here: 229 us
  other arithmetic  92.4 us (40%)
  waiting for transfers between devices  57 us (24%)
  starting transfers between devices  37 us (16%)
  matrix products  30.9 us (13%)
  local copies, waits for them, and re-layouts  10.5 us (5%)
    all_to_all x1, waiting for transfers between devices, sum_at_owner(): parts = lax.all_to_all(cut_along(shard, dim, peers), axis, 0, 0, tiled=True)  39.6 us
    concatenate x1, other arithmetic, transform_tables(): jnp.concatenate([jnp.concatenate([back_re, back_im], 1), jnp.concatenate(...  18.6 us
    concatenate x1, other arithmetic, transform_tables(): jnp.concatenate([jnp.concatenate([spec_re, spec_im], 1), jnp.concatenate(...  18.1 us
    dot_general x8, matrix products, hsum(): jnp.einsum(form, left, right, precision=HIGHEST, preferred_element_type=j...  14.8 us
    dot_general x16, matrix products, hdot(): jnp.dot(left, right, precision=HIGHEST, preferred_element_type=jnp.float32)  13.2 us
    all_to_all x2, waiting for transfers between devices, from_everyone(): return lax.all_to_all(copies, axis, split_axis=0, concat_axis=0, tiled=True)  11.3 us
    all_to_all x1, starting transfers between devices, local(): lax.all_to_all(mine, 'facet', split_axis=1, concat_axis=1, tiled=True)  9.44 us
    all_to_all x1, starting transfers between devices, sum_at_owner(): parts = lax.all_to_all(cut_along(shard, dim, peers), axis, 0, 0, tiled=True)  9.15 us
  transfers between devices with their start and end apart: 6, of which 5 were waited for; matrix products, arithmetic and copies ran while one was open for 18% of the time, Pallas kernels for 0%

commit v1 on v0

--- a/solution.py
+++ b/solution.py
@@ -244,12 +244,20 @@
     phase_cos, phase_sin = facet_phase(jnp.arange(block_rows, dtype=jnp.int32), facet_offsets)
     back_re = (phase_cos * total_back[:, None, 0] + phase_sin * total_back[:, None, 1]) * norm
     back_im = (phase_cos * total_back[:, None, 1] - phase_sin * total_back[:, None, 0]) * norm
-    arrived = lax.all_to_all(
-        jnp.stack([back_re, back_im], 2).astype(jnp.bfloat16),
-        "facet",
-        split_axis=1,
-        concat_axis=1,
-        tiled=True,
+    arrived = jnp.concatenate(
+        lax.all_to_all(
+            jnp.stack(
+                jnp.split(
+                    jnp.stack([back_re, back_im], 2).astype(jnp.bfloat16),
+                    lax.axis_size("facet"),
+                    axis=1,
+                )
+            ),
+            "facet",
+            0,
+            0,
+        ),
+        axis=1,
     ).astype(jnp.float32)
     part_re = w_re
     part_im = w_im

time: 233 us -> 239 us (1.026)
  other arithmetic: 92.4 us -> 101 us
  matrix products: 30.9 us -> 26.7 us
    unnamed x0 -> x15, other arithmetic: none -> 9.48 us
    dot_general x8, matrix products: 14.8 us -> 10.6 us  [hsum(): jnp.einsum(form, left, right, precision=HIGHEST, preferred_element_type=j...]
  transfers between devices with their start and end apart: 6 -> 6, of which waited for: 5 -> 5; matrix products, arithmetic and copies ran while one was open for 18% -> 17% of each run, Pallas kernels for 0% -> 0%
where the time goes in v1:
time: 239 us; the launch traced here: 236 us
  other arithmetic  101 us (42%)
  waiting for transfers between devices  58.4 us (24%)
  starting transfers between devices  36.9 us (15%)
  matrix products  26.7 us (11%)
  local copies, waits for them, and re-layouts  10.6 us (4%)
    all_to_all x1, waiting for transfers between devices, sum_at_owner(): parts = lax.all_to_all(cut_along(shard, dim, peers), axis, 0, 0, tiled=True)  39.6 us
    concatenate x1, other arithmetic, transform_tables(): jnp.concatenate([jnp.concatenate([back_re, back_im], 1), jnp.concatenate(...  18.6 us
    concatenate x1, other arithmetic, transform_tables(): jnp.concatenate([jnp.concatenate([spec_re, spec_im], 1), jnp.concatenate(...  18.1 us
    dot_general x16, matrix products, hdot(): jnp.dot(left, right, precision=HIGHEST, preferred_element_type=jnp.float32)  13.2 us
    all_to_all x2, waiting for transfers between devices, from_everyone(): return lax.all_to_all(copies, axis, split_axis=0, concat_axis=0, tiled=True)  11.3 us
    dot_general x8, matrix products, hsum(): jnp.einsum(form, left, right, precision=HIGHEST, preferred_element_type=j...  10.6 us
    unnamed x15, other arithmetic  9.48 us
    all_to_all x1, starting transfers between devices, local(): lax.all_to_all(mine, 'facet', split_axis=1, concat_axis=1, tiled=True)  9.44 us
  transfers between devices with their start and end apart: 6, of which 5 were waited for; matrix products, arithmetic and copies ran while one was open for 17% of the time, Pallas kernels for 0%

profile of v1, /device:TPU:1, one launch (start us, length us, event | category | flops | bytes accessed | tf_op | source)
XLA Modules:
  0.0 235.9 jit_solution(14208395100464343898)
XLA Ops:
  0.0 8.5 %multiply_convert_fusion.2 = (bf16[4096,128]{0,1:T(8,128)(2,1)S(1)}, bf16[4096,128]{0,1:T(8,128)(2,1)S(1)}) fusion(), kind=kLoop, calls=%fused_computation.112 | loop fusion | flops 9961472 | bytes 2097152 | tf_op jit(solution)/shard_map/convert_element_type | solution.py:62
  8.5 7.9 %fusion.68 = bf16[4096,128]{0,1:T(8,128)(2,1)S(1)} fusion(), kind=kLoop, calls=%fused_computation.165 | loop fusion | flops 10485760 | bytes 1048576 | tf_op jit(solution)/shard_map/neg | solution.py:64
  16.4 0.7 gather_fusion.1
  17.7 1.9 fusion.126
  19.6 1.5 bitcast_convert_fusion.1
  21.1 1.2 gather_fusion
  22.4 0.7 iota_add_fusion.2
  23.1 18.1 %maximum_maximum_fusion = bf16[8192,256]{0,1:T(8,128)(2,1)S(1)} fusion(bf16[4096,128]{0,1:T(8,128)(2,1)S(1)} %get-tuple-element.313, bf16[4096,128]{0,1:T(8,128)(2,1)S(1)} %fusion.68, bf16[4096,128]{0,1:T(8,128)(2,1)S(1)} %get-tuple-element.312), kind=kLoop, calls=%fused_computation.51 | loop fusion | flops 16777216 | bytes 7340032 | tf_op jit(solution)/shard_map/concatenate | solution.py:63
  41.7 1.5 fusion.36
  43.2 1.9 fusion.158
  45.2 1.9 fusion.159
  47.1 1.9 convolution_subtract_fusion
  49.0 1.9 convolution_add_fusion.1
  51.2 1.5 copy.70
  52.8 9.1 %all-to-all-start = ((f32[8,16,16,2,128]{4,1,2,3,0:T(8,128)}), f32[8,16,16,2,128]{4,1,2,3,0:T(8,128)S(1)}, u32[]{:S(2)}, u32[]{:S(2)}) async-start(f32[8,16,16,2,128]{4,1,2,3,0:T(8,128)} %copy.70), calls=%async_computation | async-start | bytes 4194304 | tf_op jit(solution)/shard_map/all_to_all | solution.py:22
  61.9 0.7 gather_fusion.2
  62.9 7.9 %fusion.69 = bf16[128,4096]{1,0:T(8,128)(2,1)S(1)} fusion(), kind=kLoop, calls=%fused_computation.166 | loop fusion | flops 9961472 | bytes 1048576 | tf_op jit(solution)/shard_map/neg | solution.py:69
  70.8 39.6 %all-to-all-done = f32[8,16,16,2,128]{4,1,2,3,0:T(8,128)S(1)} async-done(((f32[8,16,16,2,128]{4,1,2,3,0:T(8,128)}), f32[8,16,16,2,128]{4,1,2,3,0:T(8,128)S(1)}, u32[]{:S(2)}, u32[]{:S(2)}) %all-to-all-start) | async-done | bytes 2097184 | tf_op jit(solution)/shard_map/all_to_all | solution.py:22
  110.5 0.7 copy.63
  111.2 9.4 %all-to-all-start.1 = ((f32[16,16,2,128]{3,0,2,1:T(8,128)}), f32[16,16,2,128]{3,0,2,1:T(8,128)S(1)}, u32[]{:S(2)}, u32[]{:S(2)}) async-start(f32[16,16,2,128]{3,0,2,1:T(8,128)} %copy.63), calls=%async_computation.1 | async-start | bytes 524288 | tf_op jit(solution)/shard_map/all_to_all | solution.py:207
  120.8 1.3 dynamic_slice.40
  122.8 4.9 %all-to-all-done.1 = f32[16,16,2,128]{3,0,2,1:T(8,128)S(1)} async-done(((f32[16,16,2,128]{3,0,2,1:T(8,128)}), f32[16,16,2,128]{3,0,2,1:T(8,128)S(1)}, u32[]{:S(2)}, u32[]{:S(2)}) %all-to-all-start.1) | async-done | bytes 262176 | tf_op jit(solution)/shard_map/all_to_all | solution.py:207
  128.4 0.7 broadcast_in_dim.9
  129.1 3.5 %all-to-all-start.2 = ((f32[8,16,2,128]{3,2,1,0:T(2,128)}), f32[8,16,2,128]{3,2,1,0:T(2,128)S(1)}, u32[]{:S(2)}, u32[]{:S(2)}) async-start(f32[8,16,2,128]{3,2,1,0:T(2,128)} %broadcast_in_dim.9), calls=%async_computation.2 | async-start | bytes 262144 | tf_op jit(solution)/shard_map/all_to_all | solution.py:34
  132.6 1.1 cosine_convert_fusion.2
  133.7 6.5 %all-to-all-done.2 = f32[8,16,2,128]{3,2,1,0:T(2,128)S(1)} async-done(((f32[8,16,2,128]{3,2,1,0:T(2,128)}), f32[8,16,2,128]{3,2,1,0:T(2,128)S(1)}, u32[]{:S(2)}, u32[]{:S(2)}) %all-to-all-start.2) | async-done | bytes 131104 | tf_op jit(solution)/shard_map/all_to_all | solution.py:34
  140.4 0.8 fusion.154
  141.3 0.8 fusion.156
  142.1 0.8 convolution_subtract_fusion.3
  143.0 0.9 fusion.155
  143.8 0.9 fusion.157
  144.7 0.8 convolution_add_fusion.4
  145.6 0.9 fusion.51
  146.5 0.9 fusion.52
  147.6 1.2 fusion.73
  148.9 5.3 %while.15 = (s32[]{:T(128)}, f32[256,512]{1,0:T(8,128)S(1)}, s32[]{:T(128)}, s32[1,2,256]{2,1,0:T(2,128)S(1)}, s32[1,1,1]{2,1,0:T(1,128)}, /*index=5*/bf16[1,256...) while((s32[]{:T(128)}, f32[256,512]{1,0:T(8,128)S(1)}, ...), condition=%wide.region_6.7_spmd.clone, body=%wide.region_5.6_spmd.clone.sunk | while | flops 141363712 | bytes 2383489 | solution.py:240
  149.6 1.3 fusion.344
  150.9 1.3 fusion.345
  152.2 1.3 cosine_convert_fusion.5
  154.2 0.8 fusion.108
  155.0 0.8 fusion.104
  155.9 0.8 convolution_add_fusion.3
  156.7 0.8 fusion.153
  157.5 0.8 convolution_subtract_fusion.2
  158.3 0.8 fusion.152
  159.1 0.8 fusion.58
  159.9 0.8 fusion.57
  160.6 0.9 broadcast_in_dim.10
  161.6 4.1 %all-to-all-start.3 = ((bf16[8,128,2,128]{3,1,2,0:T(8,128)(2,1)}), bf16[8,128,2,128]{3,1,2,0:T(8,128)(2,1)}, u32[]{:S(2)}, u32[]{:S(2)}) async-start(bf16[8,128,2,128]{3,1,2,0:T(8,128)(2,1)} %broadcast_in_dim.10), calls=%async_computation.3 | async-start | bytes 1048576 | tf_op jit(solution)/shard_map/all_to_all | solution.py:34
  165.7 1.9 fusion.120
  167.6 8.5 %multiply_convert_fusion = (bf16[128,4096]{1,0:T(8,128)(2,1)S(1)}, bf16[128,4096]{1,0:T(8,128)(2,1)S(1)}) fusion(), kind=kLoop, calls=%fused_computation.108 | loop fusion | flops 9437184 | bytes 2097152 | tf_op jit(solution)/shard_map/convert_element_type | solution.py:67
  176.1 4.8 %all-to-all-done.3 = bf16[8,128,2,128]{3,1,2,0:T(8,128)(2,1)} async-done(((bf16[8,128,2,128]{3,1,2,0:T(8,128)(2,1)}), bf16[8,128,2,128]{3,1,2,0:T(8,128)(2,1)}, u32[]{:S(2)}, u32[]{:S(2)}) %all-to-all-start.3) | async-done | bytes 524320 | tf_op jit(solution)/shard_map/all_to_all | solution.py:34
  180.9 1.1 convert_reduce_fusion
  182.1 4.8 %multiply_convert_fusion.5 = (bf16[128,16,1,128]{3,0,2,1:T(8,128)(2,1)S(1)}, bf16[128,16,1,128]{3,0,2,1:T(8,128)(2,1)S(1)}) fusion(f32[128,128]{1,0:T(8,128)S(1)} %get-tuple-element.295, f32[128,128]{1,0:T(8,128)S(1)} %get-tuple-element.294, s32[16,128]{1,0:T(8,128)S(1)} %add_select_fusion.15, s32[128,16]{0,1:T(8,128)S(1)} %add_select_fusion.16), kind=kLoop, calls=%fused_computation.154 | loop fusion | flops 6291456 | bytes 1196032 | tf_op jit(solution)/shard_map/convert.7
  197.0 8.2 %all-to-all-start.4 = ((bf16[16,128,1,2,128]{4,1,3,2,0:T(8,128)(2,1)}), bf16[16,128,1,2,128]{4,1,3,2,0:T(8,128)(2,1)}, u32[]{:S(2)}, u32[]{:S(2)}) async-start(bf16[16,128,1,2,128]{4,1,3,2,0:T(8,128)(2,1)} %fusion.149), calls=%async_computation.4 | async-start | bytes 2097152 | tf_op jit(solution)/shard_map/all_to_all | solution.py:248
  205.2 18.6 %maximum_maximum_fusion.1 = bf16[256,8192]{1,0:T(8,128)(2,1)} fusion(bf16[128,4096]{1,0:T(8,128)(2,1)S(1)} %get-tuple-element.315, bf16[128,4096]{1,0:T(8,128)(2,1)S(1)} %fusion.69, bf16[128,4096]{1,0:T(8,128)(2,1)S(1)} %get-tuple-element.314), kind=kLoop, calls=%fused_computation.52 | loop fusion | flops 16777216 | bytes 7340032 | tf_op jit(solution)/shard_map/concatenate | solution.py:68
  223.8 1.4 copy.77
  225.2 0.7 fusion.66
  225.9 0.7 fusion.67
  226.7 0.7 fusion.60
  227.4 0.7 fusion.59
  228.2 2.5 %collective-permute-start = (bf16[128,256]{1,0:T(8,128)(2,1)S(1)}, bf16[128,256]{1,0:T(8,128)(2,1)S(1)}, u32[]{:S(2)}, u32[]{:S(2)}) collective-permute-start(bf16[128,256]{1,0:T(8,128)(2,1)S(1)} %copy_bitcast_fusion.1), channel_id=1, source_target_pairs={{0,1},{1,0},{2,3},{3,2},{4,5},{5,4},{6,7},{7,6},{8,9},{9,8},{10,11... | collective-permute-start | bytes 196616 | tf_op jit(solution)/shard_map/ppermute | solution.py:48
  230.9 2.5 %collective-permute-done = bf16[128,256]{1,0:T(8,128)(2,1)S(1)} collective-permute-done((bf16[128,256]{1,0:T(8,128)(2,1)S(1)}, bf16[128,256]{1,0:T(8,128)(2,1)S(1)}, u32[]{:S(2)}, u32[]{:S(2)}) %collective-permute-start) | collective-permute-done | bytes 65568 | tf_op jit(solution)/shard_map/ppermute | solution.py:48
  233.5 0.7 fusion.39
  (81 shorter events, 15.9 us)
Async XLA Ops:
  0.0 62.7 %copy-start = (s32[1,2,1,2,256]{4,3,2,1,0:T(2,128)S(1)}, s32[1,2,1,2,256]{4,3,2,1,0:T(2,128)}, u32[]{:S(2)}) copy-start(s32[1,2,1,2,256]{4,3,2,1,0:T(2,128)} %param.14) | copy-start | bytes 12292
  0.0 16.4 %copy-start.1 = (s32[32,2]{0,1:T(2,128)S(1)}, s32[32,2]{0,1:T(2,128)}, u32[]{:S(2)}) copy-start(s32[32,2]{0,1:T(2,128)} %param.11) | copy-start | bytes 772
  17.1 0.6 copy-start.8
  23.1 25.9 %copy-start.6 = (s32[8]{0:T(128)}, s32[8]{0:T(128)S(1)}, u32[]{:S(2)}) copy-start(s32[8]{0:T(128)S(1)} %iota_add_fusion.4) | copy-start | bytes 100
  23.1 18.1 %copy-start.4 = (f32[16,4096]{1,0:T(8,128)S(1)}, f32[16,4096]{1,0:T(8,128)}, u32[]{:S(2)}) copy-start(f32[16,4096]{1,0:T(8,128)} %get-tuple-element.309) | copy-start | bytes 786436
  23.1 18.1 %copy-start.5 = (f32[8,4096]{1,0:T(8,128)S(1)}, f32[8,4096]{1,0:T(8,128)}, u32[]{:S(2)}) copy-start(f32[8,4096]{1,0:T(8,128)} %get-tuple-element.299) | copy-start | bytes 393220
  52.7 9.9 %copy-start.10 = (bf16[1,2,1,256]{3,1,2,0:T(2,128)(2,1)S(1)}, bf16[1,2,1,256]{3,1,2,0:T(2,128)(2,1)}, u32[]{:S(2)}) copy-start(bf16[1,2,1,256]{3,1,2,0:T(2,128)(2,1)} %param.16) | copy-start | bytes 3076
  52.7 9.9 %copy-start.12 = (bf16[1,2,1,2,256]{4,3,2,1,0:T(2,128)(2,1)S(1)}, bf16[1,2,1,2,256]{4,3,2,1,0:T(2,128)(2,1)}, u32[]{:S(2)}) copy-start(bf16[1,2,1,2,256]{4,3,2,1,0:T(2,128)(2,1)} %param.15) | copy-start | bytes 6148
  52.8 9.9 %copy-start.11 = (s32[16,2]{0,1:T(2,128)S(1)}, s32[16,2]{0,1:T(2,128)}, u32[]{:S(2)}) copy-start(s32[16,2]{0,1:T(2,128)} %param.12) | copy-start | bytes 388
  52.8 57.6 %all-to-all-start = ((f32[8,16,16,2,128]{4,1,2,3,0:T(8,128)}), f32[8,16,16,2,128]{4,1,2,3,0:T(8,128)S(1)}, u32[]{:S(2)}, u32[]{:S(2)}) async-start(f32[8,16,16,2,128]{4,1,2,3,0:T(8,128)} %copy.70), calls=%async_computation | async-start | bytes 4194304 | tf_op jit(solution)/shard_map/all_to_all | solution.py:22
  62.9 57.8 %copy-start.9 = (s32[16]{0:T(128)S(1)}, s32[16]{0:T(128)}, u32[]{:S(2)}) copy-start(s32[16]{0:T(128)} %copy-done.8) | copy-start | bytes 196
  111.2 16.5 %all-to-all-start.1 = ((f32[16,16,2,128]{3,0,2,1:T(8,128)}), f32[16,16,2,128]{3,0,2,1:T(8,128)S(1)}, u32[]{:S(2)}, u32[]{:S(2)}) async-start(f32[16,16,2,128]{3,0,2,1:T(8,128)} %copy.63), calls=%async_computation.1 | async-start | bytes 524288 | tf_op jit(solution)/shard_map/all_to_all | solution.py:207
  129.1 16.5 %copy-start.13 = (bf16[1,2,256,256]{3,2,1,0:T(8,128)(2,1)S(1)}, bf16[1,2,256,256]{3,2,1,0:T(8,128)(2,1)}, u32[]{:S(2)}) copy-start(bf16[1,2,256,256]{3,2,1,0:T(8,128)(2,1)} %param.13) | copy-start | bytes 786436
  129.1 11.2 %all-to-all-start.2 = ((f32[8,16,2,128]{3,2,1,0:T(2,128)}), f32[8,16,2,128]{3,2,1,0:T(2,128)S(1)}, u32[]{:S(2)}, u32[]{:S(2)}) async-start(f32[8,16,2,128]{3,2,1,0:T(2,128)} %broadcast_in_dim.9), calls=%async_computation.2 | async-start | bytes 262144 | tf_op jit(solution)/shard_map/all_to_all | solution.py:34
  161.6 19.4 %all-to-all-start.3 = ((bf16[8,128,2,128]{3,1,2,0:T(8,128)(2,1)}), bf16[8,128,2,128]{3,1,2,0:T(8,128)(2,1)}, u32[]{:S(2)}, u32[]{:S(2)}) async-start(bf16[8,128,2,128]{3,1,2,0:T(8,128)(2,1)} %broadcast_in_dim.10), calls=%async_computation.3 | async-start | bytes 1048576 | tf_op jit(solution)/shard_map/all_to_all | solution.py:34
  197.0 26.8 %all-to-all-start.4 = ((bf16[16,128,1,2,128]{4,1,3,2,0:T(8,128)(2,1)}), bf16[16,128,1,2,128]{4,1,3,2,0:T(8,128)(2,1)}, u32[]{:S(2)}, u32[]{:S(2)}) async-start(bf16[16,128,1,2,128]{4,1,3,2,0:T(8,128)(2,1)} %fusion.149), calls=%async_computation.4 | async-start | bytes 2097152 | tf_op jit(solution)/shard_map/all_to_all | solution.py:248
  223.8 1.5 copy-start.7
  223.8 6.9 %copy-start.2 = (bf16[256,8192]{1,0:T(8,128)(2,1)S(1)}, bf16[256,8192]{1,0:T(8,128)(2,1)}, u32[]{:S(2)}) copy-start(bf16[256,8192]{1,0:T(8,128)(2,1)} %maximum_maximum_fusion.1) | copy-start | bytes 12582916
  228.2 5.3 %collective-permute-start = (bf16[128,256]{1,0:T(8,128)(2,1)S(1)}, bf16[128,256]{1,0:T(8,128)(2,1)S(1)}, u32[]{:S(2)}, u32[]{:S(2)}) collective-permute-start(bf16[128,256]{1,0:T(8,128)(2,1)S(1)} %copy_bitcast_fusion.1), channel_id=1, source_target_pairs={{0,1},{1,0},{2,3},{3,2},{4,5},{5,4},{6,7},{7,6},{8,9},{9,8},{10,11... | collective-permute-start | bytes 196616 | tf_op jit(solution)/shard_map/ppermute | solution.py:48
  233.5 1.0 copy-start.3
